TPU v7x, 512 devices: a whole 4x4x16 slice. The times are simulated.
512 devices in a mesh: rows: 512 (over z, x, y, core).
Axes of the slice: x: 4, y: 4, z: 16, core: 2. Of those that a mesh axis runs over, the one named last changes fastest.
Arguments:
- signal: bfloat16 [524288, 256], P('rows'), may hold values from -6 to 6
- leaves: bfloat16 [524288, 512], P('rows'), may hold values from -0.25 to 0.25
- bases: bfloat16 [4, 524288, 128], P(None, 'rows'), may hold values from -6 to 6
- couplings: bfloat16 [15, 128, 128], replicated, may hold values from -0.5 to 0.5
- weights: float32 [524288], P('rows'), may hold values from 0.25 to 4
Outputs:
- result: bfloat16 [524288, 256], P('rows')
All inputs are finite; a program needn't handle non-finite values.
Results may differ from a plain program's by a relative error of at most 0.007.
Values sent between devices are 32-bit elements; how exact they have to be, the bound alone decides.
A program may use at most 64 MiB of HBM per device.

v0:
```python
import math

import jax
import jax.numpy as jnp
from jax import lax
from jax.sharding import PartitionSpec as P

LEAF = 512


def partner(value, axis, apart):
    mask = 2**apart
    pairs = [(source, source ^ mask) for source in range(lax.axis_size(axis))]
    return lax.ppermute(value, axis, pairs)


def on_device(signal, leaves, bases, couplings, weights):
    count = lax.axis_size("rows")
    bits = count.bit_length() - 1
    myself = lax.axis_index("rows")
    rows_dev = signal.shape[0]
    width = signal.shape[1]
    rank = bases.shape[2]
    levels = bases.shape[0]

    def sums_doubling(proj):
        totals = proj
        siblings = [None] * levels
        for step in range(bits):
            active = min(levels, bits - step)
            keeping = min(levels, bits - step - 1)
            got = partner(totals, "rows", step)
            if active > keeping:
                siblings[active - 1] = got[active - 1]
            totals = totals[:keeping] + got[:keeping]
        return siblings

    def apply_kernel(vec):
        nleaf = rows_dev // LEAF
        result = jnp.einsum(
            "lab,lbc->lac",
            leaves.reshape(nleaf, LEAF, LEAF),
            vec.reshape(nleaf, LEAF, width),
            preferred_element_type=jnp.float32,
        ).reshape(rows_dev, width)
        proj = jnp.einsum("lrk,rc->lkc", bases, vec, preferred_element_type=jnp.float32)
        siblings = sums_doubling(proj)
        for level in range(levels):
            level_bit = bits - level - 1
            side = myself >> level_bit & 1
            pair_idx = myself >> level_bit + 1
            size = rows_dev * (count >> level + 1)
            factor = 1.0 / math.sqrt(size * rank)
            quotient = (siblings[level] * factor).astype(jnp.bfloat16)
            coupling = lax.dynamic_index_in_dim(
                couplings, (1 << level) - 1 + pair_idx, 0, keepdims=False
            )
            oriented = jnp.where(side == 0, coupling, coupling.T)
            coeffs = jnp.dot(oriented, quotient, preferred_element_type=jnp.float32).astype(
                jnp.bfloat16
            )
            result = result + jnp.dot(bases[level], coeffs, preferred_element_type=jnp.float32)
        return result

    first = apply_kernel(signal)
    scaled = (weights[:, None] * first).astype(jnp.bfloat16)
    return apply_kernel(scaled).astype(jnp.bfloat16)


def solution(mesh):
    in_specs = (P("rows", None), P("rows", None), P(None, "rows", None), P(), P("rows"))
    out_specs = P("rows", None)
    return jax.shard_map(
        on_device, mesh=mesh, in_specs=in_specs, out_specs=out_specs, check_vma=False
    )
```

profile of v0, /device:TPU:1, one launch (start us, length us, event | category | flops | bytes accessed | tf_op | source)
XLA Modules:
  0.0 308.7 jit_solution(7574774479410315499)
XLA Ops:
  1.9 8.7 %collective-permute-start = (f32[4,128,256]{2,1,0:T(8,128)S(1)}, f32[4,128,256]{2,1,0:T(8,128)S(1)}, u32[]{:S(2)}, u32[]{:S(2)}) collective-permute-start(f32[4,128,256]{2,1,0:T(8,128)S(1)} %fusion.14), channel_id=1, source_target_pairs={{0,1},{1,0},{2,3},{3,2},{4,5},{5,4},{6,7},{7,6},{8,9},{9,8},{10,11... | collective-permute-start | bytes 1572872 | tf_op jit(solution)/shard_map/ppermute | solution.py:14
  14.2 13.1 %collective-permute-done.1 = f32[4,128,256]{2,1,0:T(8,128)S(1)} collective-permute-done((f32[4,128,256]{2,1,0:T(8,128)S(1)}, f32[4,128,256]{2,1,0:T(8,128)S(1)}, u32[]{:S(2)}, u32[]{:S(2)}) %collective-permute-start.1) | collective-permute-done | bytes 524320 | tf_op jit(solution)/shard_map/ppermute | solution.py:14
  29.3 13.7 %collective-permute-done.2 = f32[4,128,256]{2,1,0:T(8,128)S(1)} collective-permute-done((f32[4,128,256]{2,1,0:T(8,128)S(1)}, f32[4,128,256]{2,1,0:T(8,128)S(1)}, u32[]{:S(2)}, u32[]{:S(2)}) %collective-permute-start.2) | collective-permute-done | bytes 524320 | tf_op jit(solution)/shard_map/ppermute | solution.py:14
  45.0 11.4 %collective-permute-done.3 = f32[4,128,256]{2,1,0:T(8,128)S(1)} collective-permute-done((f32[4,128,256]{2,1,0:T(8,128)S(1)}, f32[4,128,256]{2,1,0:T(8,128)S(1)}, u32[]{:S(2)}, u32[]{:S(2)}) %collective-permute-start.3) | collective-permute-done | bytes 524320 | tf_op jit(solution)/shard_map/ppermute | solution.py:14
  58.4 12.0 %collective-permute-done.4 = f32[4,128,256]{2,1,0:T(8,128)S(1)} collective-permute-done((f32[4,128,256]{2,1,0:T(8,128)S(1)}, f32[4,128,256]{2,1,0:T(8,128)S(1)}, u32[]{:S(2)}, u32[]{:S(2)}) %collective-permute-start.4) | collective-permute-done | bytes 524320 | tf_op jit(solution)/shard_map/ppermute | solution.py:14
  72.5 9.7 %collective-permute-done.5 = f32[4,128,256]{2,1,0:T(8,128)S(1)} collective-permute-done((f32[4,128,256]{2,1,0:T(8,128)S(1)}, f32[4,128,256]{2,1,0:T(8,128)S(1)}, u32[]{:S(2)}, u32[]{:S(2)}) %collective-permute-start.5) | collective-permute-done | bytes 524320 | tf_op jit(solution)/shard_map/ppermute | solution.py:14
  90.4 2.4 convolution_bitcast_fusion.4
  92.8 11.9 %collective-permute-done.6 = f32[3,128,256]{2,1,0:T(8,128)} collective-permute-done((f32[3,128,256]{2,1,0:T(8,128)S(1)}, f32[3,128,256]{2,1,0:T(8,128)}, u32[]{:S(2)}, u32[]{:S(2)}) %collective-permute-start.6) | collective-permute-done | bytes 393248 | tf_op jit(solution)/shard_map/ppermute | solution.py:14
  105.7 4.1 %collective-permute-start.7 = (f32[2,128,256]{2,1,0:T(8,128)S(1)}, f32[2,128,256]{2,1,0:T(8,128)S(1)}, u32[]{:S(2)}, u32[]{:S(2)}) collective-permute-start(f32[2,128,256]{2,1,0:T(8,128)S(1)} %slice_add_fusion.3), channel_id=1, source_target_pairs={{0,128},{1,129},{2,130},{3,131},{4,132},{5,133},{6,134},{7,135},{8... | collective-permute-start | bytes 786440 | tf_op jit(solution)/shard_map/ppermute | solution.py:14
  109.8 2.4 convolution_bitcast_fusion.5
  112.2 21.5 %collective-permute-done.7 = f32[2,128,256]{2,1,0:T(8,128)S(1)} collective-permute-done((f32[2,128,256]{2,1,0:T(8,128)S(1)}, f32[2,128,256]{2,1,0:T(8,128)S(1)}, u32[]{:S(2)}, u32[]{:S(2)}) %collective-permute-start.7) | collective-permute-done | bytes 262176 | tf_op jit(solution)/shard_map/ppermute | solution.py:14
  133.8 14.1 %collective-permute-start.8 = (f32[1,128,256]{2,1,0:T(8,128)S(1)}, f32[1,128,256]{2,1,0:T(8,128)S(1)}, u32[]{:S(2)}, u32[]{:S(2)}) collective-permute-start(f32[1,128,256]{2,1,0:T(8,128)S(1)} %slice_add_fusion.5), channel_id=1, source_target_pairs={{0,256},{1,257},{2,258},{3,259},{4,260},{5,261},{6,262},{7,263},{8... | collective-permute-start | bytes 393224 | tf_op jit(solution)/shard_map/ppermute | solution.py:14
  149.4 3.7 %collective-permute-done.8 = f32[1,128,256]{2,1,0:T(8,128)S(1)} collective-permute-done((f32[1,128,256]{2,1,0:T(8,128)S(1)}, f32[1,128,256]{2,1,0:T(8,128)S(1)}, u32[]{:S(2)}, u32[]{:S(2)}) %collective-permute-start.8) | collective-permute-done | bytes 131104 | tf_op jit(solution)/shard_map/ppermute | solution.py:14
  153.2 2.7 fusion.10
  156.4 2.4 collective-permute-start.9
  160.4 3.2 %collective-permute-start.10 = (f32[4,128,256]{2,1,0:T(8,128)S(1)}, f32[4,128,256]{2,1,0:T(8,128)S(1)}, u32[]{:S(2)}, u32[]{:S(2)}) collective-permute-start(f32[4,128,256]{2,1,0:T(8,128)S(1)} %add.126), channel_id=1, source_target_pairs={{0,2},{1,3},{2,0},{3,1},{4,6},{5,7},{6,4},{7,5},{8,10},{9,11},{10,... | collective-permute-start | bytes 1572872 | tf_op jit(solution)/shard_map/ppermute | solution.py:14
  163.6 11.8 %collective-permute-done.10 = f32[4,128,256]{2,1,0:T(8,128)S(1)} collective-permute-done((f32[4,128,256]{2,1,0:T(8,128)S(1)}, f32[4,128,256]{2,1,0:T(8,128)S(1)}, u32[]{:S(2)}, u32[]{:S(2)}) %collective-permute-start.10) | collective-permute-done | bytes 524320 | tf_op jit(solution)/shard_map/ppermute | solution.py:14
  175.5 4.8 %collective-permute-start.11 = (f32[4,128,256]{2,1,0:T(8,128)S(1)}, f32[4,128,256]{2,1,0:T(8,128)S(1)}, u32[]{:S(2)}, u32[]{:S(2)}) collective-permute-start(f32[4,128,256]{2,1,0:T(8,128)S(1)} %add.127), channel_id=1, source_target_pairs={{0,4},{1,5},{2,6},{3,7},{4,0},{5,1},{6,2},{7,3},{8,12},{9,13},{10,... | collective-permute-start | bytes 1572872 | tf_op jit(solution)/shard_map/ppermute | solution.py:14
  180.3 10.8 %collective-permute-done.11 = f32[4,128,256]{2,1,0:T(8,128)S(1)} collective-permute-done((f32[4,128,256]{2,1,0:T(8,128)S(1)}, f32[4,128,256]{2,1,0:T(8,128)S(1)}, u32[]{:S(2)}, u32[]{:S(2)}) %collective-permute-start.11) | collective-permute-done | bytes 524320 | tf_op jit(solution)/shard_map/ppermute | solution.py:14
  191.2 3.1 %collective-permute-start.12 = (f32[4,128,256]{2,1,0:T(8,128)S(1)}, f32[4,128,256]{2,1,0:T(8,128)S(1)}, u32[]{:S(2)}, u32[]{:S(2)}) collective-permute-start(f32[4,128,256]{2,1,0:T(8,128)S(1)} %add.128), channel_id=1, source_target_pairs={{0,8},{1,9},{2,10},{3,11},{4,12},{5,13},{6,14},{7,15},{8,0},{9,1},... | collective-permute-start | bytes 1572872 | tf_op jit(solution)/shard_map/ppermute | solution.py:14
  194.4 10.2 %collective-permute-done.12 = f32[4,128,256]{2,1,0:T(8,128)S(1)} collective-permute-done((f32[4,128,256]{2,1,0:T(8,128)S(1)}, f32[4,128,256]{2,1,0:T(8,128)S(1)}, u32[]{:S(2)}, u32[]{:S(2)}) %collective-permute-start.12) | collective-permute-done | bytes 524320 | tf_op jit(solution)/shard_map/ppermute | solution.py:14
  204.6 4.7 %collective-permute-start.13 = (f32[4,128,256]{2,1,0:T(8,128)S(1)}, f32[4,128,256]{2,1,0:T(8,128)S(1)}, u32[]{:S(2)}, u32[]{:S(2)}) collective-permute-start(f32[4,128,256]{2,1,0:T(8,128)S(1)} %add.129), channel_id=1, source_target_pairs={{0,16},{1,17},{2,18},{3,19},{4,20},{5,21},{6,22},{7,23},{8,24},{9,... | collective-permute-start | bytes 1572872 | tf_op jit(solution)/shard_map/ppermute | solution.py:14
  209.2 9.3 %collective-permute-done.13 = f32[4,128,256]{2,1,0:T(8,128)S(1)} collective-permute-done((f32[4,128,256]{2,1,0:T(8,128)S(1)}, f32[4,128,256]{2,1,0:T(8,128)S(1)}, u32[]{:S(2)}, u32[]{:S(2)}) %collective-permute-start.13) | collective-permute-done | bytes 524320 | tf_op jit(solution)/shard_map/ppermute | solution.py:14
  220.5 9.7 %collective-permute-done.14 = f32[4,128,256]{2,1,0:T(8,128)S(1)} collective-permute-done((f32[4,128,256]{2,1,0:T(8,128)S(1)}, f32[4,128,256]{2,1,0:T(8,128)S(1)}, u32[]{:S(2)}, u32[]{:S(2)}) %collective-permute-start.14) | collective-permute-done | bytes 524320 | tf_op jit(solution)/shard_map/ppermute | solution.py:14
  237.2 2.4 convolution_bitcast_fusion
  239.6 13.1 %collective-permute-done.15 = f32[3,128,256]{2,1,0:T(8,128)} collective-permute-done((f32[3,128,256]{2,1,0:T(8,128)S(1)}, f32[3,128,256]{2,1,0:T(8,128)}, u32[]{:S(2)}, u32[]{:S(2)}) %collective-permute-start.15) | collective-permute-done | bytes 393248 | tf_op jit(solution)/shard_map/ppermute | solution.py:14
  254.4 6.1 %collective-permute-start.16 = (f32[2,128,256]{2,1,0:T(8,128)}, f32[2,128,256]{2,1,0:T(8,128)S(1)}, u32[]{:S(2)}, u32[]{:S(2)}) collective-permute-start(f32[2,128,256]{2,1,0:T(8,128)} %slice_add_fusion.2), channel_id=1, source_target_pairs={{0,128},{1,129},{2,130},{3,131},{4,132},{5,133},{6,134},{7,135},{8... | collective-permute-start | bytes 786440 | tf_op jit(solution)/shard_map/ppermute | solution.py:14
  260.5 2.4 convolution_bitcast_fusion.1
  262.9 21.4 %collective-permute-done.16 = f32[2,128,256]{2,1,0:T(8,128)S(1)} collective-permute-done((f32[2,128,256]{2,1,0:T(8,128)}, f32[2,128,256]{2,1,0:T(8,128)S(1)}, u32[]{:S(2)}, u32[]{:S(2)}) %collective-permute-start.16) | collective-permute-done | bytes 262176 | tf_op jit(solution)/shard_map/ppermute | solution.py:14
  285.9 8.6 %collective-permute-start.17 = (f32[1,128,256]{2,1,0:T(8,128)}, f32[1,128,256]{2,1,0:T(8,128)}, u32[]{:S(2)}, u32[]{:S(2)}) collective-permute-start(f32[1,128,256]{2,1,0:T(8,128)} %slice_add_fusion.4), channel_id=1, source_target_pairs={{0,256},{1,257},{2,258},{3,259},{4,260},{5,261},{6,262},{7,263},{8... | collective-permute-start | bytes 393224 | tf_op jit(solution)/shard_map/ppermute | solution.py:14
  296.0 7.5 %collective-permute-done.17 = f32[1,128,256]{2,1,0:T(8,128)} collective-permute-done((f32[1,128,256]{2,1,0:T(8,128)}, f32[1,128,256]{2,1,0:T(8,128)}, u32[]{:S(2)}, u32[]{:S(2)}) %collective-permute-start.17) | collective-permute-done | bytes 131104 | tf_op jit(solution)/shard_map/ppermute | solution.py:14
  303.5 3.2 %fusion.9 = bf16[1024,256]{0,1:T(8,128)(2,1)} fusion(f32[1024,256]{0,1:T(8,128)} %convolution_bitcast_fusion, f32[1024,256]{0,1:T(8,128)} %convolution_bitcast_fusion.1, f32[1024,256]{0,1:T(8,128)} %convolution_bitcast_fusion.2, f32[1024,256]{0,1:T(8,128)S(1)} %copy-done.2, bf16[4,1024,128]{2,1,0:T(8,128)(2,1)S(1)} %copy-done.1, ...), kind=kOutput, calls=%fused_computation.18 | convolution fusion | flops 76922880 | bytes 5177345 | tf_op jit(solution)/shard_map/dot_general | solution.py:62
  (87 shorter events, 42.3 us)
Async XLA Ops:
  0.0 84.9 %copy-start = (bf16[1024,512]{1,0:T(8,128)(2,1)S(1)}, bf16[1024,512]{1,0:T(8,128)(2,1)}, u32[]{:S(2)}) copy-start(bf16[1024,512]{1,0:T(8,128)(2,1)} %param.6) | copy-start | bytes 3145732
  1.9 10.3 %collective-permute-start = (f32[4,128,256]{2,1,0:T(8,128)S(1)}, f32[4,128,256]{2,1,0:T(8,128)S(1)}, u32[]{:S(2)}, u32[]{:S(2)}) collective-permute-start(f32[4,128,256]{2,1,0:T(8,128)S(1)} %fusion.14), channel_id=1, source_target_pairs={{0,1},{1,0},{2,3},{3,2},{4,5},{5,4},{6,7},{7,6},{8,9},{9,8},{10,11... | collective-permute-start | bytes 1572872 | tf_op jit(solution)/shard_map/ppermute | solution.py:14
  12.3 15.0 %collective-permute-start.1 = (f32[4,128,256]{2,1,0:T(8,128)S(1)}, f32[4,128,256]{2,1,0:T(8,128)S(1)}, u32[]{:S(2)}, u32[]{:S(2)}) collective-permute-start(f32[4,128,256]{2,1,0:T(8,128)S(1)} %add.108), channel_id=1, source_target_pairs={{0,2},{1,3},{2,0},{3,1},{4,6},{5,7},{6,4},{7,5},{8,10},{9,11},{10,... | collective-permute-start | bytes 1572872 | tf_op jit(solution)/shard_map/ppermute | solution.py:14
  27.3 15.7 %collective-permute-start.2 = (f32[4,128,256]{2,1,0:T(8,128)S(1)}, f32[4,128,256]{2,1,0:T(8,128)S(1)}, u32[]{:S(2)}, u32[]{:S(2)}) collective-permute-start(f32[4,128,256]{2,1,0:T(8,128)S(1)} %add.109), channel_id=1, source_target_pairs={{0,4},{1,5},{2,6},{3,7},{4,0},{5,1},{6,2},{7,3},{8,12},{9,13},{10,... | collective-permute-start | bytes 1572872 | tf_op jit(solution)/shard_map/ppermute | solution.py:14
  43.1 13.3 %collective-permute-start.3 = (f32[4,128,256]{2,1,0:T(8,128)S(1)}, f32[4,128,256]{2,1,0:T(8,128)S(1)}, u32[]{:S(2)}, u32[]{:S(2)}) collective-permute-start(f32[4,128,256]{2,1,0:T(8,128)S(1)} %add.110), channel_id=1, source_target_pairs={{0,8},{1,9},{2,10},{3,11},{4,12},{5,13},{6,14},{7,15},{8,0},{9,1},... | collective-permute-start | bytes 1572872 | tf_op jit(solution)/shard_map/ppermute | solution.py:14
  56.4 13.9 %collective-permute-start.4 = (f32[4,128,256]{2,1,0:T(8,128)S(1)}, f32[4,128,256]{2,1,0:T(8,128)S(1)}, u32[]{:S(2)}, u32[]{:S(2)}) collective-permute-start(f32[4,128,256]{2,1,0:T(8,128)S(1)} %add.111), channel_id=1, source_target_pairs={{0,16},{1,17},{2,18},{3,19},{4,20},{5,21},{6,22},{7,23},{8,24},{9,... | collective-permute-start | bytes 1572872 | tf_op jit(solution)/shard_map/ppermute | solution.py:14
  70.5 11.7 %collective-permute-start.5 = (f32[4,128,256]{2,1,0:T(8,128)S(1)}, f32[4,128,256]{2,1,0:T(8,128)S(1)}, u32[]{:S(2)}, u32[]{:S(2)}) collective-permute-start(f32[4,128,256]{2,1,0:T(8,128)S(1)} %add.112), channel_id=1, source_target_pairs={{0,32},{1,33},{2,34},{3,35},{4,36},{5,37},{6,38},{7,39},{8,40},{9,... | collective-permute-start | bytes 1572872 | tf_op jit(solution)/shard_map/ppermute | solution.py:14
  83.0 21.7 %collective-permute-start.6 = (f32[3,128,256]{2,1,0:T(8,128)S(1)}, f32[3,128,256]{2,1,0:T(8,128)}, u32[]{:S(2)}, u32[]{:S(2)}) collective-permute-start(f32[3,128,256]{2,1,0:T(8,128)S(1)} %slice_add_fusion.1), channel_id=1, source_target_pairs={{0,64},{1,65},{2,66},{3,67},{4,68},{5,69},{6,70},{7,71},{8,72},{9,... | collective-permute-start | bytes 1179656 | tf_op jit(solution)/shard_map/ppermute | solution.py:14
  92.8 17.0 %copy-start.20 = (bf16[128,128]{0,1:T(8,128)(2,1)S(1)}, bf16[128,128]{0,1:T(8,128)(2,1)}, u32[]{:S(2)}) copy-start(bf16[128,128]{0,1:T(8,128)(2,1)} %copy.19) | copy-start | bytes 98308
  105.7 28.0 %collective-permute-start.7 = (f32[2,128,256]{2,1,0:T(8,128)S(1)}, f32[2,128,256]{2,1,0:T(8,128)S(1)}, u32[]{:S(2)}, u32[]{:S(2)}) collective-permute-start(f32[2,128,256]{2,1,0:T(8,128)S(1)} %slice_add_fusion.3), channel_id=1, source_target_pairs={{0,128},{1,129},{2,130},{3,131},{4,132},{5,133},{6,134},{7,135},{8... | collective-permute-start | bytes 786440 | tf_op jit(solution)/shard_map/ppermute | solution.py:14
  112.2 35.8 %copy-start.8 = (bf16[128,128]{1,0:T(8,128)(2,1)S(1)}, bf16[128,128]{1,0:T(8,128)(2,1)}, u32[]{:S(2)}) copy-start(bf16[128,128]{1,0:T(8,128)(2,1)} %copy-done.7) | copy-start | bytes 98308
  112.2 35.8 %copy-start.18 = (bf16[128,128]{0,1:T(8,128)(2,1)S(1)}, bf16[128,128]{0,1:T(8,128)(2,1)}, u32[]{:S(2)}) copy-start(bf16[128,128]{0,1:T(8,128)(2,1)} %copy.18) | copy-start | bytes 98308
  133.7 19.4 %copy-start.5 = (bf16[128,128]{1,0:T(8,128)(2,1)S(1)}, bf16[128,128]{1,0:T(8,128)(2,1)}, u32[]{:S(2)}) copy-start(bf16[128,128]{1,0:T(8,128)(2,1)} %copy-done.4) | copy-start | bytes 98308
  133.7 19.4 %copy-start.16 = (bf16[128,128]{0,1:T(8,128)(2,1)S(1)}, bf16[128,128]{0,1:T(8,128)(2,1)}, u32[]{:S(2)}) copy-start(bf16[128,128]{0,1:T(8,128)(2,1)} %copy.15) | copy-start | bytes 98308
  133.8 19.4 %copy-start.22 = (f32[1024]{0:T(1024)S(1)}, f32[1024]{0:T(1024)}, u32[]{:S(2)}) copy-start(f32[1024]{0:T(1024)} %param.9) | copy-start | bytes 12292
  133.8 19.4 %collective-permute-start.8 = (f32[1,128,256]{2,1,0:T(8,128)S(1)}, f32[1,128,256]{2,1,0:T(8,128)S(1)}, u32[]{:S(2)}, u32[]{:S(2)}) collective-permute-start(f32[1,128,256]{2,1,0:T(8,128)S(1)} %slice_add_fusion.5), channel_id=1, source_target_pairs={{0,256},{1,257},{2,258},{3,259},{4,260},{5,261},{6,262},{7,263},{8... | collective-permute-start | bytes 393224 | tf_op jit(solution)/shard_map/ppermute | solution.py:14
  156.4 3.9 %collective-permute-start.9 = (f32[4,128,256]{2,1,0:T(8,128)S(1)}, f32[4,128,256]{2,1,0:T(8,128)S(1)}, u32[]{:S(2)}, u32[]{:S(2)}) collective-permute-start(f32[4,128,256]{2,1,0:T(8,128)S(1)} %convolution_bitcast_fusion.9), channel_id=1, source_target_pairs={{0,1},{1,0},{2,3},{3,2},{4,5},{5,4},{6,7},{7,6},{8,9},{9,8},{10,11... | collective-permute-start | bytes 1572872 | tf_op jit(solution)/shard_map/ppermute | solution.py:14
  160.4 15.0 %collective-permute-start.10 = (f32[4,128,256]{2,1,0:T(8,128)S(1)}, f32[4,128,256]{2,1,0:T(8,128)S(1)}, u32[]{:S(2)}, u32[]{:S(2)}) collective-permute-start(f32[4,128,256]{2,1,0:T(8,128)S(1)} %add.126), channel_id=1, source_target_pairs={{0,2},{1,3},{2,0},{3,1},{4,6},{5,7},{6,4},{7,5},{8,10},{9,11},{10,... | collective-permute-start | bytes 1572872 | tf_op jit(solution)/shard_map/ppermute | solution.py:14
  175.5 15.7 %collective-permute-start.11 = (f32[4,128,256]{2,1,0:T(8,128)S(1)}, f32[4,128,256]{2,1,0:T(8,128)S(1)}, u32[]{:S(2)}, u32[]{:S(2)}) collective-permute-start(f32[4,128,256]{2,1,0:T(8,128)S(1)} %add.127), channel_id=1, source_target_pairs={{0,4},{1,5},{2,6},{3,7},{4,0},{5,1},{6,2},{7,3},{8,12},{9,13},{10,... | collective-permute-start | bytes 1572872 | tf_op jit(solution)/shard_map/ppermute | solution.py:14
  191.2 13.3 %collective-permute-start.12 = (f32[4,128,256]{2,1,0:T(8,128)S(1)}, f32[4,128,256]{2,1,0:T(8,128)S(1)}, u32[]{:S(2)}, u32[]{:S(2)}) collective-permute-start(f32[4,128,256]{2,1,0:T(8,128)S(1)} %add.128), channel_id=1, source_target_pairs={{0,8},{1,9},{2,10},{3,11},{4,12},{5,13},{6,14},{7,15},{8,0},{9,1},... | collective-permute-start | bytes 1572872 | tf_op jit(solution)/shard_map/ppermute | solution.py:14
  204.6 13.9 %collective-permute-start.13 = (f32[4,128,256]{2,1,0:T(8,128)S(1)}, f32[4,128,256]{2,1,0:T(8,128)S(1)}, u32[]{:S(2)}, u32[]{:S(2)}) collective-permute-start(f32[4,128,256]{2,1,0:T(8,128)S(1)} %add.129), channel_id=1, source_target_pairs={{0,16},{1,17},{2,18},{3,19},{4,20},{5,21},{6,22},{7,23},{8,24},{9,... | collective-permute-start | bytes 1572872 | tf_op jit(solution)/shard_map/ppermute | solution.py:14
  218.6 11.6 %collective-permute-start.14 = (f32[4,128,256]{2,1,0:T(8,128)S(1)}, f32[4,128,256]{2,1,0:T(8,128)S(1)}, u32[]{:S(2)}, u32[]{:S(2)}) collective-permute-start(f32[4,128,256]{2,1,0:T(8,128)S(1)} %add.130), channel_id=1, source_target_pairs={{0,32},{1,33},{2,34},{3,35},{4,36},{5,37},{6,38},{7,39},{8,40},{9,... | collective-permute-start | bytes 1572872 | tf_op jit(solution)/shard_map/ppermute | solution.py:14
  231.0 21.7 %collective-permute-start.15 = (f32[3,128,256]{2,1,0:T(8,128)S(1)}, f32[3,128,256]{2,1,0:T(8,128)}, u32[]{:S(2)}, u32[]{:S(2)}) collective-permute-start(f32[3,128,256]{2,1,0:T(8,128)S(1)} %slice_add_fusion), channel_id=1, source_target_pairs={{0,64},{1,65},{2,66},{3,67},{4,68},{5,69},{6,70},{7,71},{8,72},{9,... | collective-permute-start | bytes 1179656 | tf_op jit(solution)/shard_map/ppermute | solution.py:14
  239.6 20.8 %copy-start.12 = (bf16[128,128]{1,0:T(8,128)(2,1)S(1)}, bf16[128,128]{1,0:T(8,128)(2,1)}, u32[]{:S(2)}) copy-start(bf16[128,128]{1,0:T(8,128)(2,1)} %copy-done.10) | copy-start | bytes 98308
  239.6 20.9 %copy-start.21 = (bf16[128,128]{0,1:T(8,128)(2,1)S(1)}, bf16[128,128]{0,1:T(8,128)(2,1)}, u32[]{:S(2)}) copy-start(bf16[128,128]{0,1:T(8,128)(2,1)} %copy.19) | copy-start | bytes 98308
  254.4 30.0 %collective-permute-start.16 = (f32[2,128,256]{2,1,0:T(8,128)}, f32[2,128,256]{2,1,0:T(8,128)S(1)}, u32[]{:S(2)}, u32[]{:S(2)}) collective-permute-start(f32[2,128,256]{2,1,0:T(8,128)} %slice_add_fusion.2), channel_id=1, source_target_pairs={{0,128},{1,129},{2,130},{3,131},{4,132},{5,133},{6,134},{7,135},{8... | collective-permute-start | bytes 786440 | tf_op jit(solution)/shard_map/ppermute | solution.py:14
  260.5 34.0 %copy-start.9 = (bf16[128,128]{1,0:T(8,128)(2,1)S(1)}, bf16[128,128]{1,0:T(8,128)(2,1)}, u32[]{:S(2)}) copy-start(bf16[128,128]{1,0:T(8,128)(2,1)} %copy-done.7) | copy-start | bytes 98308
  260.5 34.0 %copy-start.19 = (bf16[128,128]{0,1:T(8,128)(2,1)S(1)}, bf16[128,128]{0,1:T(8,128)(2,1)}, u32[]{:S(2)}) copy-start(bf16[128,128]{0,1:T(8,128)(2,1)} %copy.18) | copy-start | bytes 98308
  262.9 40.6 %copy-start.2 = (f32[1024,256]{0,1:T(8,128)S(1)}, f32[1024,256]{0,1:T(8,128)}, u32[]{:S(2)}) copy-start(f32[1024,256]{0,1:T(8,128)} %copy.24) | copy-start | bytes 3145732
  285.9 17.6 %copy-start.6 = (bf16[128,128]{1,0:T(8,128)(2,1)S(1)}, bf16[128,128]{1,0:T(8,128)(2,1)}, u32[]{:S(2)}) copy-start(bf16[128,128]{1,0:T(8,128)(2,1)} %copy-done.4) | copy-start | bytes 98308
  285.9 17.6 %copy-start.17 = (bf16[128,128]{0,1:T(8,128)(2,1)S(1)}, bf16[128,128]{0,1:T(8,128)(2,1)}, u32[]{:S(2)}) copy-start(bf16[128,128]{0,1:T(8,128)(2,1)} %copy.15) | copy-start | bytes 98308
  285.9 17.6 %collective-permute-start.17 = (f32[1,128,256]{2,1,0:T(8,128)}, f32[1,128,256]{2,1,0:T(8,128)}, u32[]{:S(2)}, u32[]{:S(2)}) collective-permute-start(f32[1,128,256]{2,1,0:T(8,128)} %slice_add_fusion.4), channel_id=1, source_target_pairs={{0,256},{1,257},{2,258},{3,259},{4,260},{5,261},{6,262},{7,263},{8... | collective-permute-start | bytes 393224 | tf_op jit(solution)/shard_map/ppermute | solution.py:14
  (9 other events, 39.4 us)
where the time goes:
time: 311 us; the launch traced here: 309 us
  waiting for transfers between devices  194 us (62%)
  starting transfers between devices  75.3 us (24%)
  matrix products  22.8 us (7%)
  local copies, waits for them, and re-layouts  11.4 us (4%)
  other arithmetic  5.04 us (2%)
    ppermute x18, waiting for transfers between devices, partner(): return lax.ppermute(value, axis, pairs)  194 us
    ppermute x18, starting transfers between devices, partner(): return lax.ppermute(value, axis, pairs)  75.3 us
    dot_general x8, matrix products, apply_kernel(): jnp.dot(bases[level], coeffs, preferred_element_type=jnp.float32)  18.5 us
  transfers between devices with their start and end apart: 18, of which 18 were waited for; matrix products, arithmetic and copies ran while one was open for 7% of the time, Pallas kernels for 0%

commit v1 on v0

v1 whole, which is shorter than its diff:
```python
import math

import jax
import jax.numpy as jnp
from jax import lax
from jax.experimental import pallas as pl
from jax.experimental.pallas import tpu as pltpu
from jax.sharding import PartitionSpec as P

LEAF = 512
NY = 4
CHIPS = 16
PLANES = 16
MESH = pl.DeviceIdType.MESH
GROUPS = ((0, 1), (1, 2), (2, 4))
F32 = jnp.float32
BF16 = jnp.bfloat16


def multi_wait(ref, sem):
    pltpu.make_async_copy(ref, ref, sem).wait()


def kernel(
    scales, x_hbm, leaves_hbm, bases_hbm, coup_hbm, w_hbm, out_ref,
    xv, bcat, lv, mraw, mor, wv, wcol, xs, acc, cb,
    p, rbuf, hs, rs, sv, zr, qt, ag, ag2,
    load_sem, send_sem, recv_sem,
):
    rows, width = xv.shape
    levels, rank = mor.shape[0], mor.shape[1]
    half = width // 2
    me = lax.axis_index("rows")
    core = me % 2
    chip = me // 2 % CHIPS
    cx, cy = chip // NY, chip % NY
    z = me // (2 * CHIPS)
    partner = me + 1 - 2 * core

    def plane_peer(d):
        q = (cx + d // NY) % NY * NY + (cy + d % NY) % NY
        return q, (z * CHIPS + q) * 2 + core

    def z_peer(level, i):
        s = (PLANES // 2) >> level
        mine = z // s
        other = mine + 1 - 2 * (mine % 2)
        zz = other * s + (z % s + i) % s
        return (zz * CHIPS + chip) * 2 + core

    loads = [pltpu.make_async_copy(x_hbm, xv, load_sem.at[0])]
    for l in range(levels):
        loads.append(pltpu.make_async_copy(
            bases_hbm.at[l], bcat.at[:, pl.ds(l * rank, rank)], load_sem.at[1 + l]))
    loads.append(pltpu.make_async_copy(leaves_hbm, lv, load_sem.at[5]))
    for l in range(levels):
        s = (PLANES // 2) >> l
        idx = (1 << l) - 1 + z // (2 * s)
        loads.append(pltpu.make_async_copy(coup_hbm.at[idx], mraw.at[l], load_sem.at[6 + l]))
    loads.append(pltpu.make_async_copy(w_hbm, wv, load_sem.at[10]))
    for c in loads:
        c.start()

    barrier = pltpu.get_barrier_semaphore()

    def tell(dev):
        pl.semaphore_signal(barrier, inc=1, device_id=(dev,), device_id_type=MESH)

    for l in range(levels):
        def tell_z(i, _):
            tell(z_peer(l, i))
            return 0
        lax.fori_loop(0, (PLANES // 2) >> l, tell_z, 0)

    def tell_plane(d, _):
        tell(plane_peer(d)[1])
        return 0
    lax.fori_loop(1, CHIPS, tell_plane, 0)
    tell(partner)

    def project(a, vec_ref):
        got = lax.dot_general(bcat[...], vec_ref[...], (((0,), (0,)), ((), ())),
                              preferred_element_type=F32)
        for h in range(2):
            for l in range(levels):
                p[a, h, l] = got[l * rank:(l + 1) * rank, h * half:(h + 1) * half]

    def remote(src, dst, a, phase, g, dev):
        pltpu.make_async_remote_copy(
            src_ref=src, dst_ref=dst, send_sem=send_sem.at[a, phase, g],
            recv_sem=recv_sem.at[a, phase, g], device_id=(dev,), device_id_type=MESH,
        ).start()

    def leaf_part(vec_ref):
        for b in range(rows // LEAF):
            sl = pl.ds(b * LEAF, LEAF)
            acc[sl, :] = jnp.dot(lv[sl, :], vec_ref[sl, :], preferred_element_type=F32)

    def coefficients(a, between):
        for g, (lo, hi) in enumerate(GROUPS):
            n = hi - lo
            remote(p.at[a, 1 - core, pl.ds(lo, n)], rbuf.at[a, pl.ds(lo, n)], a, 0, g, partner)
        for g, (lo, hi) in enumerate(GROUPS):
            n = hi - lo
            multi_wait(rbuf.at[a, pl.ds(lo, n)], recv_sem.at[a, 0, g])
            hs[a, lo:hi] = p[a, core, lo:hi] + rbuf[a, lo:hi]

            def send_rs(d, _):
                q, dev = plane_peer(d)
                remote(hs.at[a, pl.ds(lo, n), pl.ds(pl.multiple_of(q * 8, 8), 8)],
                       rs.at[a, d - 1, pl.ds(lo, n)], a, 1, g, dev)
                return 0
            lax.fori_loop(1, CHIPS, send_rs, 0)
        between()
        mine = pl.ds(pl.multiple_of(chip * 8, 8), 8)
        for g, (lo, hi) in enumerate(GROUPS):
            n = hi - lo
            multi_wait(rs.at[a, :, pl.ds(lo, n)], recv_sem.at[a, 1, g])
            total = hs[a, lo:hi, mine, :]
            for d in range(CHIPS - 1):
                total = total + rs[a, d, lo:hi]
            sv[a, lo:hi] = total
            for l in range(lo, hi):
                s = (PLANES // 2) >> l

                def send_z(i, _):
                    remote(sv.at[a, l], zr.at[a, s + i], a, 2, l, z_peer(l, i))
                    return 0
                lax.fori_loop(0, s, send_z, 0)
        for g, (lo, hi) in reversed(list(enumerate(GROUPS))):
            n = hi - lo
            for l in range(lo, hi):
                s = (PLANES // 2) >> l
                multi_wait(zr.at[a, pl.ds(s, s)], recv_sem.at[a, 2, l])
                total = zr[a, s]
                for i in range(1, s):
                    total = total + zr[a, s + i]
                total = total * scales[l]
                qt[a, l] = total
                ag[a, l, mine, :] = total

            def send_ag(d, _):
                q, dev = plane_peer(d)
                remote(qt.at[a, pl.ds(lo, n)], ag.at[a, pl.ds(lo, n), mine], a, 3, g, dev)
                return 0
            lax.fori_loop(1, CHIPS, send_ag, 0)
        for g, (lo, hi) in reversed(list(enumerate(GROUPS))):
            n = hi - lo
            multi_wait(ag.at[a, pl.ds(lo, n), pl.ds(0, 8 * (CHIPS - 1))], recv_sem.at[a, 3, g])
            remote(ag.at[a, pl.ds(lo, n)], ag2.at[a, pl.ds(lo, n)], a, 4, g, partner)
            for l in range(lo, hi):
                got = jnp.dot(mor[l], ag[a, l].astype(BF16), preferred_element_type=F32)
                cb[l * rank:(l + 1) * rank,
                   pl.ds(pl.multiple_of(core * half, half), half)] = got.astype(BF16)
        for g, (lo, hi) in reversed(list(enumerate(GROUPS))):
            n = hi - lo
            multi_wait(ag2.at[a, pl.ds(lo, n)], recv_sem.at[a, 4, g])
            for l in range(lo, hi):
                got = jnp.dot(mor[l], ag2[a, l].astype(BF16), preferred_element_type=F32)
                cb[l * rank:(l + 1) * rank,
                   pl.ds(pl.multiple_of((1 - core) * half, half), half)] = got.astype(BF16)

    for c in loads[:5]:
        c.wait()
    project(0, xv)
    pl.semaphore_wait(barrier, 2 * CHIPS - 1)

    def early():
        for c in loads[5:]:
            c.wait()
        leaf_part(xv)
        for l in range(levels):
            s = (PLANES // 2) >> l
            side = z // s % 2
            m = mraw[l].astype(F32)
            mor[l] = jnp.where(side == 0, m, m.T).astype(BF16)
        for r in range(rows // 128):
            row = jnp.broadcast_to(wv[r:r + 1, :], (128, 128))
            wcol[r * 128:(r + 1) * 128, :] = row.T

    coefficients(0, early)
    first = acc[...] + jnp.dot(bcat[...], cb[...], preferred_element_type=F32)
    for h in range(2):
        hl = slice(h * half, (h + 1) * half)
        xs[:, hl] = (wcol[...] * first[:, hl]).astype(BF16)
    project(1, xs)
    coefficients(1, lambda: leaf_part(xs))
    out_ref[...] = (acc[...] + jnp.dot(bcat[...], cb[...], preferred_element_type=F32)).astype(BF16)

    for a in range(2):
        for g, (lo, hi) in enumerate(GROUPS):
            n = hi - lo
            multi_wait(rbuf.at[a, pl.ds(lo, n)], send_sem.at[a, 0, g])
            multi_wait(rs.at[a, :, pl.ds(lo, n)], send_sem.at[a, 1, g])
            multi_wait(ag.at[a, pl.ds(lo, n), pl.ds(0, 8 * (CHIPS - 1))], send_sem.at[a, 3, g])
            multi_wait(ag2.at[a, pl.ds(lo, n)], send_sem.at[a, 4, g])
        for l in range(levels):
            s = (PLANES // 2) >> l
            multi_wait(zr.at[a, pl.ds(s, s)], send_sem.at[a, 2, l])


def on_device(signal, leaves, bases, couplings, weights):
    rows, width = signal.shape
    levels, _, rank = bases.shape
    count = lax.axis_size("rows")
    scales = [1.0 / math.sqrt(rows * (count >> level + 1) * rank) for level in range(levels)]
    half = width // 2
    vm = pltpu.VMEM
    anyspec = pl.BlockSpec(memory_space=pl.ANY)
    dma = pltpu.SemaphoreType.DMA

    def body(*refs):
        kernel(scales, *refs)

    return pl.pallas_call(
        body,
        name="double_product",
        out_shape=jax.ShapeDtypeStruct((rows, width), BF16),
        in_specs=[anyspec] * 5,
        out_specs=pl.BlockSpec(memory_space=vm),
        scratch_shapes=[
            vm((rows, width), BF16),
            vm((rows, levels * rank), BF16),
            vm((rows, LEAF), BF16),
            vm((levels, rank, rank), BF16),
            vm((levels, rank, rank), BF16),
            vm((rows // 128, 128), F32),
            vm((rows, 128), F32),
            vm((rows, width), BF16),
            vm((rows, width), F32),
            vm((levels * rank, width), BF16),
            vm((2, 2, levels, rank, half), F32),
            vm((2, levels, rank, half), F32),
            vm((2, levels, rank, half), F32),
            vm((2, CHIPS - 1, levels, 8, half), F32),
            vm((2, levels, 8, half), F32),
            vm((2, PLANES, 8, half), F32),
            vm((2, levels, 8, half), F32),
            vm((2, levels, rank, half), F32),
            vm((2, levels, rank, half), F32),
            dma((11,)),
            dma((2, 5, 4)),
            dma((2, 5, 4)),
        ],
        compiler_params=pltpu.CompilerParams(collective_id=0, has_side_effects=True),
    )(signal, leaves, bases, couplings, weights.reshape(rows // 128, 128))


def solution(mesh):
    in_specs = (P("rows", None), P("rows", None), P(None, "rows", None), P(), P("rows"))
    return jax.shard_map(
        on_device, mesh=mesh, in_specs=in_specs, out_specs=P("rows", None), check_vma=False
    )
```

time: 311 us -> 62.2 us (0.20)
  waiting for transfers between devices: 194 us -> 0 us
  starting transfers between devices: 75.3 us -> 0 us
  Pallas kernels: 0 us -> 60.1 us
  matrix products: 22.8 us -> 0 us
  local copies, waits for them, and re-layouts: 11.4 us -> 1.87 us
  other arithmetic: 5.04 us -> 0 us
    ppermute x18 -> x0, waiting for transfers between devices: 194 us -> none  [partner(): return lax.ppermute(value, axis, pairs)]
    ppermute x18 -> x0, starting transfers between devices: 75.3 us -> none  [partner(): return lax.ppermute(value, axis, pairs)]
    pallas_call x0 -> x1, Pallas kernels: none -> 60.1 us  [on_device(): pl.pallas_call(body, name='double_product', out_shape=jax.ShapeDtypeStruc...]
    dot_general x12 -> x0, matrix products: 22.8 us -> none  [the longest x8 18.5 us: apply_kernel(): jnp.dot(bases[level], coeffs, preferred_element_type=jnp.float32)]
    add x16 -> x0, other arithmetic: 5.04 us -> none  [sums_doubling(): totals = totals[:keeping] + got[:keeping]]
    squeeze x5 -> x0, local copies, waits for them, and re-layouts: 3.66 us -> none  [apply_kernel(): lax.dynamic_index_in_dim(couplings, (1 << level) - 1 + pair_idx, 0, keepd...]
  transfers between devices with their start and end apart: 18 -> 0, of which waited for: 18 -> 0; matrix products, arithmetic and copies ran while one was open for 7% -> 0% of each run, Pallas kernels for 0% -> 0%
where the time goes in v1:
time: 62.2 us; the launch traced here: 62 us
  Pallas kernels  60.1 us (97%)
  local copies, waits for them, and re-layouts  1.87 us (3%)
    pallas_call x1, Pallas kernels, on_device(): pl.pallas_call(body, name='double_product', out_shape=jax.ShapeDtypeStruc...  60.1 us
    unnamed x1, local copies, waits for them, and re-layouts  1.87 us

profile of v1, /device:TPU:1, one launch (start us, length us, event | category | flops | bytes accessed | tf_op | source)
XLA Modules:
  0.0 62.0 jit_solution(56780628164011583)
XLA Ops:
  0.0 60.1 %double_product.1 = bf16[1024,256]{1,0:T(8,128)(2,1)} custom-call(bf16[1024,256]{1,0:T(8,128)(2,1)} %refs_0_.1, bf16[1024,512]{1,0:T(8,128)(2,1)} %refs_1_.1, bf16[4,1024,128]{2,1,0:T(8,128)(2,1)} %refs_2_.1, bf16[15,128,128]{2,1,0:T(8,128)(2,1)} %refs_3_.1, f32[8,128]{1,0:T(8,128)} %bitcast.1), custom_call_target="tpu_custom_call" | custom-call | tf_op jit(solution)/shard_map/double_product/pallas_call | solution.py:215
  60.1 1.9 %copy.7 = bf16[1024,256]{1,0:T(8,128)(2,1)} copy(bf16[1024,256]{1,0:T(8,128)(2,1)} %double_product.1) | data formatting | bytes 1048576

commit v2 on v1

v2 whole, which is shorter than its diff:
```python
import math

import jax
import jax.numpy as jnp
from jax import lax
from jax.experimental import pallas as pl
from jax.experimental.pallas import tpu as pltpu
from jax.sharding import PartitionSpec as P

LEAF = 512
NY = 4
CHIPS = 16
PLANES = 16
MESH = pl.DeviceIdType.MESH
GROUPS = ((0, 1), (1, 2), (2, 4))
GRAM_FIRST = True
F32 = jnp.float32
BF16 = jnp.bfloat16


def multi_wait(ref, sem):
    pltpu.make_async_copy(ref, ref, sem).wait()
ORDER = tuple(reversed(tuple(enumerate(GROUPS))))
PAIR_P, RS_P, Z0, AG0, FWD0, PAIR_U, RS_U, PAIR_G, RS_G, PAIR_R, Z1, AG1, FWD1 = range(13)
TN = (((0,), (0,)), ((), ()))


def multi_wait(ref, sem):
    pltpu.make_async_copy(ref, ref, sem).wait()


def kernel(
    scales, x_hbm, leaves_hbm, bases_hbm, coup_hbm, w_hbm, out_ref,
    xv, bcat, lv, mraw, mor, wv, wcol, wb, ys, xs, acc, cb, ch,
    p, rbuf, hs, rs, u, ubuf, us, urs, g, gbuf, gs, grs, gm, gx, ghl, usum,
    sv, zr, qt, ag, ag2,
    load_sem, send_sem, recv_sem, round_sem,
):
    rows, width = xv.shape
    levels, rank = mor.shape[0], mor.shape[1]
    half = width // 2
    me = lax.axis_index("rows")
    core = me % 2
    chip = me // 2 % CHIPS
    cx, cy = chip // NY, chip % NY
    z = me // (2 * CHIPS)
    partner = me + 1 - 2 * core
    mine = pl.ds(pl.multiple_of(chip * 8, 8), 8)
    own_cols = pl.ds(pl.multiple_of(core * half, half), half)
    other_cols = pl.ds(pl.multiple_of((1 - core) * half, half), half)

    def plane_peer(d):
        q = (cx + d // NY) % NY * NY + (cy + d % NY) % NY
        return q, (z * CHIPS + q) * 2 + core

    def along_z(d):
        return ((z + d + PLANES) % PLANES * CHIPS + chip) * 2 + core

    def z_peer(level, i):
        s = (PLANES // 2) >> level
        side = z // s
        other = side + 1 - 2 * (side % 2)
        zz = other * s + (z % s + i) % s
        return (zz * CHIPS + chip) * 2 + core

    loads = [pltpu.make_async_copy(x_hbm, xv, load_sem.at[0])]
    for l in range(levels):
        loads.append(pltpu.make_async_copy(
            bases_hbm.at[l], bcat.at[:, pl.ds(l * rank, rank)], load_sem.at[1 + l]))
    loads.append(pltpu.make_async_copy(leaves_hbm, lv, load_sem.at[5]))
    for l in range(levels):
        s = (PLANES // 2) >> l
        idx = (1 << l) - 1 + z // (2 * s)
        loads.append(pltpu.make_async_copy(coup_hbm.at[idx], mraw.at[l], load_sem.at[6 + l]))
    loads.append(pltpu.make_async_copy(w_hbm, wv, load_sem.at[10]))
    for c in loads:
        c.start()

    barrier = pltpu.get_barrier_semaphore()

    def tell(dev):
        pl.semaphore_signal(barrier, inc=1, device_id=(dev,), device_id_type=MESH)

    def tell_plane(d, _):
        tell(plane_peer(d)[1])
        return 0
    lax.fori_loop(1, CHIPS, tell_plane, 0)
    tell(partner)
    for d in (1, -1):
        tell(along_z(d))

    def z_round(r):
        for d in (1 << r, -(1 << r)):
            pl.semaphore_signal(round_sem.at[r], inc=1, device_id=(along_z(d),), device_id_type=MESH)

    sent = []

    def remote(src, dst, phase, grp, dev):
        pltpu.make_async_remote_copy(
            src_ref=src, dst_ref=dst, send_sem=send_sem.at[phase, grp],
            recv_sem=recv_sem.at[phase, grp], device_id=(dev,), device_id_type=MESH,
        ).start()

    def arrived(ref, phase, grp):
        multi_wait(ref, recv_sem.at[phase, grp])
        sent.append((ref, phase, grp))

    def project(vec_ref, dst):
        got = lax.dot_general(bcat[...], vec_ref[...], TN, preferred_element_type=F32)
        for h in range(2):
            for l in range(levels):
                dst[h, l] = got[l * rank:(l + 1) * rank, h * half:(h + 1) * half]

    def leaf_part(vec_ref):
        for b in range(rows // LEAF):
            sl = pl.ds(b * LEAF, LEAF)
            acc[sl, :] = jnp.dot(lv[sl, :], vec_ref[sl, :], preferred_element_type=F32)

    def scatter(src, dst, phase, grp, lo, hi):
        def body(d, _):
            q, dev = plane_peer(d)
            remote(src.at[pl.ds(lo, hi - lo), pl.ds(pl.multiple_of(q * 8, 8), 8)],
                   dst.at[d - 1, pl.ds(lo, hi - lo)], phase, grp, dev)
            return 0
        lax.fori_loop(1, CHIPS, body, 0)

    def gathered_sum(src, buf, lo, hi):
        total = src[lo:hi, mine, :]
        for d in range(CHIPS - 1):
            total = total + buf[d, lo:hi]
        return total

    def z_send(a, l):
        s = (PLANES // 2) >> l

        def body(i, _):
            remote(sv.at[a, l], zr.at[a, s + i], (Z0, Z1)[a], l, z_peer(l, i))
            return 0
        lax.fori_loop(0, s, body, 0)

    def z_to_gather(a):
        for grp, (lo, hi) in ORDER:
            for l in range(lo, hi):
                s = (PLANES // 2) >> l
                arrived(zr.at[a, pl.ds(s, s)], (Z0, Z1)[a], l)
                total = zr[a, s]
                for i in range(1, s):
                    total = total + zr[a, s + i]
                total = total * scales[l]
                qt[a, l] = total
                ag[a, l, mine, :] = total

            def body(d, _):
                _, dev = plane_peer(d)
                remote(qt.at[a, pl.ds(lo, hi - lo)], ag.at[a, pl.ds(lo, hi - lo), mine],
                       (AG0, AG1)[a], grp, dev)
                return 0
            lax.fori_loop(1, CHIPS, body, 0)

    def couple(l, buf, cols):
        got = jnp.dot(mor[l], buf[l].astype(BF16), preferred_element_type=F32).astype(BF16)
        cb[l * rank:(l + 1) * rank, cols] = got
        return got

    def own_half(a):
        for grp, (lo, hi) in ORDER:
            arrived(ag.at[a, pl.ds(lo, hi - lo), pl.ds(0, 8 * (CHIPS - 1))], (AG0, AG1)[a], grp)
            remote(ag.at[a, pl.ds(lo, hi - lo)], ag2.at[a, pl.ds(lo, hi - lo)],
                   (FWD0, FWD1)[a], grp, partner)
            for l in range(lo, hi):
                ch[l * rank:(l + 1) * rank, :] = couple(l, ag.at[a], own_cols)

    def other_half(a):
        for grp, (lo, hi) in ORDER:
            arrived(ag2.at[a, pl.ds(lo, hi - lo)], (FWD0, FWD1)[a], grp)
            for l in range(lo, hi):
                couple(l, ag2.at[a], other_cols)

    for c in loads[:5]:
        c.wait()
    project(xv, p)
    pl.semaphore_wait(barrier, CHIPS + 2)
    for grp, (lo, hi) in enumerate(GROUPS):
        remote(p.at[1 - core, pl.ds(lo, hi - lo)], rbuf.at[pl.ds(lo, hi - lo)], PAIR_P, grp, partner)
    z_round(0)

    loads[10].wait()
    for r in range(rows // 128):
        row = jnp.broadcast_to(wv[r:r + 1, :], (128, 128))
        wcol[r * 128:(r + 1) * 128, :] = row.T
    for l in range(levels):
        cl = slice(l * rank, (l + 1) * rank)
        wb[:, cl] = (wcol[...] * bcat[:, cl].astype(F32)).astype(BF16)

    def gram():
        got = lax.dot_general(bcat[...], wb[...], TN, preferred_element_type=F32)
        for h in range(2):
            for l in range(levels):
                g[h, l] = got[l * rank:(l + 1) * rank, h * 2 * rank:(h + 1) * 2 * rank]
        remote(g.at[1 - core], gbuf, PAIR_G, 0, partner)

    if GRAM_FIRST:
        gram()
    for grp, (lo, hi) in enumerate(GROUPS):
        arrived(rbuf.at[pl.ds(lo, hi - lo)], PAIR_P, grp)
        hs[lo:hi] = p[core, lo:hi] + rbuf[lo:hi]
        scatter(hs, rs, RS_P, grp, lo, hi)
    if not GRAM_FIRST:
        gram()
    pl.semaphore_wait(round_sem.at[0], 2)
    z_round(1)

    loads[5].wait()
    leaf_part(xv)
    for h in range(2):
        hl = slice(h * half, (h + 1) * half)
        ys[:, hl] = (wcol[...] * acc[:, hl]).astype(BF16)
    project(ys, u)
    remote(u.at[1 - core], ubuf, PAIR_U, 0, partner)
    pl.semaphore_wait(round_sem.at[1], 2)
    z_round(2)
    arrived(gbuf, PAIR_G, 0)
    gs[...] = g[core] + gbuf[...]
    scatter(gs, grs, RS_G, 0, 0, levels)
    arrived(ubuf, PAIR_U, 0)
    us[...] = u[core] + ubuf[...]
    scatter(us, urs, RS_U, 0, 0, levels)

    pl.semaphore_wait(round_sem.at[2], 2)
    for grp, (lo, hi) in enumerate(GROUPS):
        arrived(rs.at[:, pl.ds(lo, hi - lo)], RS_P, grp)
        sv[0, lo:hi] = gathered_sum(hs, rs, lo, hi)
        for l in range(lo, hi):
            z_send(0, l)

    for c in loads[6:10]:
        c.wait()
    for l in range(levels):
        s = (PLANES // 2) >> l
        side = z // s % 2
        m = mraw[l].astype(F32)
        mor[l] = jnp.where(side == 0, m, m.T).astype(BF16)

    z_to_gather(0)
    arrived(grs, RS_G, 0)
    gm[...] = gathered_sum(gs, grs, 0, levels)
    remote(gm, gx, PAIR_R, 0, partner)
    arrived(urs, RS_U, 0)
    usum[...] = gathered_sum(us, urs, 0, levels)
    arrived(gx, PAIR_R, 0)
    for k in range(2):
        full = jnp.where(core == k, gm[...], gx[...]).reshape(levels * 8, 2 * rank)
        hi_part = full.astype(BF16)
        ghl[0, k] = hi_part
        ghl[1, k] = (full - hi_part.astype(F32)).astype(BF16)

    own_half(0)
    nxt = usum[...].reshape(levels * 8, half)
    for k in range(2):
        cols = ch[k * 2 * rank:(k + 1) * 2 * rank, :]
        for part in range(2):
            nxt = nxt + jnp.dot(ghl[part, k], cols, preferred_element_type=F32)
    sv[1] = nxt.reshape(levels, 8, half)
    for l in range(levels):
        z_send(1, l)

    other_half(0)
    first = acc[...] + jnp.dot(bcat[...], cb[...], preferred_element_type=F32)
    for h in range(2):
        hl = slice(h * half, (h + 1) * half)
        xs[:, hl] = (wcol[...] * first[:, hl]).astype(BF16)
    leaf_part(xs)

    z_to_gather(1)
    own_half(1)
    other_half(1)
    out_ref[...] = (acc[...] + jnp.dot(bcat[...], cb[...], preferred_element_type=F32)).astype(BF16)
    for ref, phase, grp in sent:
        multi_wait(ref, send_sem.at[phase, grp])


def on_device(signal, leaves, bases, couplings, weights):
    rows, width = signal.shape
    levels, _, rank = bases.shape
    count = lax.axis_size("rows")
    scales = [1.0 / math.sqrt(rows * (count >> level + 1) * rank) for level in range(levels)]
    half = width // 2
    vm = pltpu.VMEM
    anyspec = pl.BlockSpec(memory_space=pl.ANY)
    dma = pltpu.SemaphoreType.DMA

    def body(*refs):
        kernel(scales, *refs)

    return pl.pallas_call(
        body,
        name="double_product",
        out_shape=vm((rows, width), BF16),
        in_specs=[anyspec] * 5,
        out_specs=pl.BlockSpec(memory_space=vm),
        scratch_shapes=[
            vm((rows, width), BF16),
            vm((rows, levels * rank), BF16),
            vm((rows, LEAF), BF16),
            vm((levels, rank, rank), BF16),
            vm((levels, rank, rank), BF16),
            vm((rows // 128, 128), F32),
            vm((rows, 128), F32),
            vm((rows, levels * rank), BF16),
            vm((rows, width), BF16),
            vm((rows, width), BF16),
            vm((rows, width), F32),
            vm((levels * rank, width), BF16),
            vm((levels * rank, half), BF16),
            vm((2, levels, rank, half), F32),
            vm((levels, rank, half), F32),
            vm((levels, rank, half), F32),
            vm((CHIPS - 1, levels, 8, half), F32),
            vm((2, levels, rank, half), F32),
            vm((levels, rank, half), F32),
            vm((levels, rank, half), F32),
            vm((CHIPS - 1, levels, 8, half), F32),
            vm((2, levels, rank, 2 * rank), F32),
            vm((levels, rank, 2 * rank), F32),
            vm((levels, rank, 2 * rank), F32),
            vm((CHIPS - 1, levels, 8, 2 * rank), F32),
            vm((levels, 8, 2 * rank), F32),
            vm((levels, 8, 2 * rank), F32),
            vm((2, 2, levels * 8, 2 * rank), BF16),
            vm((levels, 8, half), F32),
            vm((2, levels, 8, half), F32),
            vm((2, PLANES, 8, half), F32),
            vm((2, levels, 8, half), F32),
            vm((2, levels, rank, half), F32),
            vm((2, levels, rank, half), F32),
            dma((11,)),
            dma((13, 4)),
            dma((13, 4)),
            pltpu.SemaphoreType.REGULAR((3,)),
        ],
        compiler_params=pltpu.CompilerParams(collective_id=0, has_side_effects=True),
    )(signal, leaves, bases, couplings, weights.reshape(rows // 128, 128))


def solution(mesh):
    in_specs = (P("rows", None), P("rows", None), P(None, "rows", None), P(), P("rows"))
    return jax.shard_map(
        on_device, mesh=mesh, in_specs=in_specs, out_specs=P("rows", None), check_vma=False
    )
```

time: 62.2 us -> 51.4 us (0.83)
  Pallas kernels: 60.1 us -> 50.5 us
  local copies, waits for them, and re-layouts: 1.87 us -> 0.8 us
    pallas_call x1, Pallas kernels: 60.1 us -> 50.5 us  [on_device(): pl.pallas_call(body, name='double_product', out_shape=vm((rows, width), B...]
    unnamed x1, local copies, waits for them, and re-layouts: 1.87 us -> 0.8 us
where the time goes in v2:
time: 51.4 us; the launch traced here: 51.3 us
  Pallas kernels  50.5 us (98%)
  local copies, waits for them, and re-layouts  0.8 us (2%)
    pallas_call x1, Pallas kernels, on_device(): pl.pallas_call(body, name='double_product', out_shape=vm((rows, width), B...  50.5 us

profile of v2, /device:TPU:1, one launch (start us, length us, event | category | flops | bytes accessed | tf_op | source)
XLA Modules:
  0.0 51.3 jit_solution(2167945283134585645)
XLA Ops:
  0.0 50.5 %double_product.1 = bf16[1024,256]{1,0:T(8,128)(2,1)S(1)} custom-call(bf16[1024,256]{1,0:T(8,128)(2,1)} %refs_0_.1, bf16[1024,512]{1,0:T(8,128)(2,1)} %refs_1_.1, bf16[4,1024,128]{2,1,0:T(8,128)(2,1)} %refs_2_.1, bf16[15,128,128]{2,1,0:T(8,128)(2,1)} %refs_3_.1, f32[8,128]{1,0:T(8,128)} %bitcast.1), custom_call_target="tpu_custom_call" | custom-call | tf_op jit(solution)/shard_map/double_product/pallas_call | solution.py:295
  50.5 0.8 %copy.7 = bf16[1024,256]{1,0:T(8,128)(2,1)} copy(bf16[1024,256]{1,0:T(8,128)(2,1)S(1)} %double_product.1) | data formatting | bytes 1048576

commit v3 on v2

v3 whole, which is shorter than its diff:
```python
import math

import jax
import jax.numpy as jnp
from jax import lax
from jax.experimental import pallas as pl
from jax.experimental.pallas import tpu as pltpu
from jax.sharding import PartitionSpec as P

LEAF = 512
NY = 4
CHIPS = 16
PLANES = 16
MESH = pl.DeviceIdType.MESH
GROUPS = ((0, 1), (1, 2), (2, 4))
F32 = jnp.float32
BF16 = jnp.bfloat16


ORDER = tuple(reversed(tuple(enumerate(GROUPS))))
OFFSETS = sorted(
    ((dx, dy) for dx in range(NY) for dy in range(NY) if dx or dy),
    key=lambda o: -min(o[0], NY - o[0]) - min(o[1], NY - o[1]),
)
PAIR_P, RS_P, Z0, AG0, FWD0, PAIR_U, RS_U, PAIR_G, RS_G, PAIR_R, Z1, AG1, FWD1 = range(13)
TN = (((0,), (0,)), ((), ()))


def multi_wait(ref, sem):
    pltpu.make_async_copy(ref, ref, sem).wait()


def kernel(
    scales, x_hbm, leaves_hbm, bases_hbm, coup_hbm, w_hbm, out_ref,
    xv, bcat, lv, mraw, mor, wv, wcol, wb, ys, xs, acc, cb,
    p, rbuf, hs, rs, rs0, u, ubuf, us, urs, g, gbuf, gs, grs, gm, gx, ghl, usum,
    sv, zr, qt, ag, ag2,
    load_sem, send_sem, recv_sem, pair_sem,
):
    rows, width = xv.shape
    levels, rank = mor.shape[0], mor.shape[1]
    half = width // 2
    me = lax.axis_index("rows")
    core = me % 2
    chip = me // 2 % CHIPS
    cx, cy = chip // NY, chip % NY
    z = me // (2 * CHIPS)
    partner = me + 1 - 2 * core
    mine = pl.ds(pl.multiple_of(chip * 8, 8), 8)
    own_cols = pl.ds(pl.multiple_of(core * half, half), half)
    other_cols = pl.ds(pl.multiple_of((1 - core) * half, half), half)

    xq = [(cx + d) % NY * NY for d in range(NY)]
    yq = [(cy + d) % NY for d in range(NY)]
    plane0 = z * (2 * CHIPS) + core
    peers = []
    for dx, dy in OFFSETS:
        q = xq[dx] + yq[dy]
        peers.append((pl.multiple_of(q * 8, 8), plane0 + q * 2))
    column0 = chip * 2 + core
    siblings = []
    for l in range(levels):
        s = (PLANES // 2) >> l
        side = z // s
        right = side % 2
        other = (side + 1 - 2 * right) * s
        devs = []
        for t in range(s):
            if l == 0:
                i = (t + 1) // 2 if t % 2 else s - t // 2
                at = (z + i) % s
            else:
                at = right * t + (1 - right) * (s - 1 - t)
            devs.append((other + at) * (2 * CHIPS) + column0)
        siblings.append((s, z % s, devs))

    hrows = rows // 2
    first_loads = []
    for r in range(2):
        rl = pl.ds(r * hrows, hrows)
        part = [pltpu.make_async_copy(x_hbm.at[rl], xv.at[rl], load_sem.at[5 * r])]
        for l in range(levels):
            part.append(pltpu.make_async_copy(
                bases_hbm.at[l, rl], bcat.at[rl, pl.ds(l * rank, rank)], load_sem.at[5 * r + 1 + l]))
        first_loads.append(part)
    w_load = pltpu.make_async_copy(w_hbm, wv, load_sem.at[10])
    leaf_load = pltpu.make_async_copy(leaves_hbm, lv, load_sem.at[11])
    m_loads = []
    for l in range(levels):
        s = (PLANES // 2) >> l
        idx = (1 << l) - 1 + z // (2 * s)
        m_loads.append(pltpu.make_async_copy(coup_hbm.at[idx], mraw.at[l], load_sem.at[12 + l]))
    for part in first_loads:
        for c in part:
            c.start()
    w_load.start()

    barrier = pltpu.get_barrier_semaphore()

    def tell(dev):
        pl.semaphore_signal(barrier, inc=1, device_id=(dev,), device_id_type=MESH)

    def tell(dev):
        pl.semaphore_signal(barrier, inc=1, device_id=(dev,), device_id_type=MESH)

    for _, _, devs in siblings:
        for dev in devs:
            tell(dev - core + 1)
    for _, dev in peers:
        tell(dev - core)
    tell(partner)

    def heard():
        pl.semaphore_wait(barrier, 2 * CHIPS - 1)
        pl.semaphore_signal(pair_sem, inc=1, device_id=(partner,), device_id_type=MESH)

    def know(heard_by):
        @pl.when(core == heard_by)
        def _():
            heard()

        @pl.when(core != heard_by)
        def _():
            pl.semaphore_wait(pair_sem, 1)

    sent = []

    def remote(src, dst, phase, grp, dev):
        pltpu.make_async_remote_copy(
            src_ref=src, dst_ref=dst, send_sem=send_sem.at[phase, grp],
            recv_sem=recv_sem.at[phase, grp], device_id=(dev,), device_id_type=MESH,
        ).start()

    def arrived(ref, phase, grp):
        multi_wait(ref, recv_sem.at[phase, grp])
        sent.append((ref, phase, grp))

    def project(vec_ref, dst):
        got = lax.dot_general(bcat[...], vec_ref[...], TN, preferred_element_type=F32)
        for h in range(2):
            for l in range(levels):
                dst[h, l] = got[l * rank:(l + 1) * rank, h * half:(h + 1) * half]

    def leaf_part(vec_ref):
        for b in range(rows // LEAF):
            sl = pl.ds(b * LEAF, LEAF)
            acc[sl, :] = jnp.dot(lv[sl, :], vec_ref[sl, :], preferred_element_type=F32)

    def scatter(src, dst, phase, grp, lo, hi):
        for d, (row, dev) in enumerate(peers):
            remote(src.at[pl.ds(lo, hi - lo), pl.ds(row, 8)], dst.at[d, pl.ds(lo, hi - lo)],
                   phase, grp, dev)

    def gathered_sum(src, buf, lo, hi):
        total = src[lo:hi, mine, :]
        for d in range(CHIPS - 1):
            total = total + buf[d, lo:hi]
        return total

    def z_send(a, l):
        s, place, devs = siblings[l]
        for dev in devs:
            remote(sv.at[a, l], zr.at[a, s + place], (Z0, Z1)[a], l, dev)

    def both_cores(a, grp):
        return a == 1 and grp == ORDER[-1][0]

    def z_to_gather(a):
        for grp, (lo, hi) in ORDER:
            for l in range(lo, hi):
                s = (PLANES // 2) >> l
                arrived(zr.at[a, pl.ds(s, s)], (Z0, Z1)[a], l)
                total = zr[a, s]
                for i in range(1, s):
                    total = total + zr[a, s + i]
                total = total * scales[l]
                qt[a, l] = total
                ag[a, l, mine, :] = total

            for _, dev in peers:
                remote(qt.at[a, pl.ds(lo, hi - lo)], ag.at[a, pl.ds(lo, hi - lo), mine],
                       (AG0, AG1)[a], grp, dev)
            if both_cores(a, grp):
                for _, dev in peers:
                    remote(qt.at[a, pl.ds(lo, hi - lo)], ag2.at[a, pl.ds(lo, hi - lo), mine],
                           (FWD0, FWD1)[a], grp, dev + 1 - 2 * core)
            if both_cores(a, grp):
                remote(qt.at[a, pl.ds(lo, hi - lo)], ag2.at[a, pl.ds(lo, hi - lo), mine],
                       (FWD0, FWD1)[a], grp, partner)

    def couple(l, buf, cols):
        got = jnp.dot(mor[l], buf[l].astype(BF16), preferred_element_type=F32).astype(BF16)
        cb[l * rank:(l + 1) * rank, cols] = got
        return got

    def own_group(a, grp, lo, hi):
        arrived(ag.at[a, pl.ds(lo, hi - lo), pl.ds(0, 8 * (CHIPS - 1))], (AG0, AG1)[a], grp)
        if not both_cores(a, grp):
            remote(ag.at[a, pl.ds(lo, hi - lo)], ag2.at[a, pl.ds(lo, hi - lo)],
                   (FWD0, FWD1)[a], grp, partner)
        return [(l, couple(l, ag.at[a], own_cols)) for l in range(lo, hi)]

    def other_group(a, grp, lo, hi):
        arrived(ag2.at[a, pl.ds(lo, hi - lo)], (FWD0, FWD1)[a], grp)
        for l in range(lo, hi):
            couple(l, ag2.at[a], other_cols)

    def expand(lo, hi):
        kl = slice(lo * rank, hi * rank)
        return jnp.dot(bcat[:, kl], cb[kl, :], preferred_element_type=F32)

    got = None
    for r in range(2):
        for c in first_loads[r]:
            c.wait()
        rl = slice(r * hrows, (r + 1) * hrows)
        more = lax.dot_general(bcat[rl, :], xv[rl, :], TN, preferred_element_type=F32)
        got = more if got is None else got + more
    for h in range(2):
        for l in range(levels):
            p[h, l] = got[l * rank:(l + 1) * rank, h * half:(h + 1) * half]
    know(0)
    for grp, (lo, hi) in enumerate(GROUPS):
        if grp == 0:
            for d, (row, dev) in enumerate(peers):
                remote(p.at[core, 0, pl.ds(row, 8)], rs0.at[d], RS_P, grp, dev)
                remote(p.at[1 - core, 0, pl.ds(row, 8)], rs0.at[CHIPS - 1 + d], RS_P, grp,
                       dev + 1 - 2 * core)
            remote(p.at[1 - core, 0, mine], rs0.at[2 * CHIPS - 2], RS_P, grp, partner)
            continue
        remote(p.at[1 - core, pl.ds(lo, hi - lo)], rbuf.at[pl.ds(lo, hi - lo)], PAIR_P, grp, partner)
    leaf_load.start()
    for c in m_loads:
        c.start()

    w_load.wait()
    for r in range(rows // 128):
        row = jnp.broadcast_to(wv[r:r + 1, :], (128, 128))
        wcol[r * 128:(r + 1) * 128, :] = row.T
    for l in range(levels):
        cl = slice(l * rank, (l + 1) * rank)
        wb[:, cl] = (wcol[...] * bcat[:, cl].astype(F32)).astype(BF16)

    def gram():
        got = lax.dot_general(bcat[...], wb[...], TN, preferred_element_type=F32)
        for h in range(2):
            for l in range(levels):
                g[h, l] = got[l * rank:(l + 1) * rank, h * 2 * rank:(h + 1) * 2 * rank]
        remote(g.at[1 - core], gbuf, PAIR_G, 0, partner)

    gram()
    for grp, (lo, hi) in enumerate(GROUPS):
        if grp == 0:
            continue
        arrived(rbuf.at[pl.ds(lo, hi - lo)], PAIR_P, grp)
        hs[lo:hi] = p[core, lo:hi] + rbuf[lo:hi]
        scatter(hs, rs, RS_P, grp, lo, hi)

    leaf_load.wait()
    leaf_part(xv)
    for h in range(2):
        hl = slice(h * half, (h + 1) * half)
        ys[:, hl] = (wcol[...] * acc[:, hl]).astype(BF16)
    project(ys, u)
    remote(u.at[1 - core], ubuf, PAIR_U, 0, partner)
    arrived(gbuf, PAIR_G, 0)
    gs[...] = g[core] + gbuf[...]
    scatter(gs, grs, RS_G, 0, 0, levels)

    know(1)
    for grp, (lo, hi) in enumerate(GROUPS):
        if grp == 0:
            arrived(rs0, RS_P, grp)
            total = p[core, 0, mine, :]
            for d in range(2 * CHIPS - 1):
                total = total + rs0[d]
            sv[0, 0] = total
        else:
            arrived(rs.at[:, pl.ds(lo, hi - lo)], RS_P, grp)
            sv[0, lo:hi] = gathered_sum(hs, rs, lo, hi)
        for l in range(lo, hi):
            z_send(0, l)

    arrived(ubuf, PAIR_U, 0)
    us[...] = u[core] + ubuf[...]
    scatter(us, urs, RS_U, 0, 0, levels)
    for c in m_loads:
        c.wait()
    for l in range(levels):
        s = (PLANES // 2) >> l
        side = z // s % 2
        m = mraw[l].astype(F32)
        mor[l] = jnp.where(side == 0, m, m.T).astype(BF16)

    z_to_gather(0)
    arrived(grs, RS_G, 0)
    gm[...] = gathered_sum(gs, grs, 0, levels)
    remote(gm, gx, PAIR_R, 0, partner)
    arrived(urs, RS_U, 0)
    usum[...] = gathered_sum(us, urs, 0, levels)
    arrived(gx, PAIR_R, 0)
    for k in range(2):
        full = jnp.where(core == k, gm[...], gx[...]).reshape(levels * 8, 2 * rank)
        hi_part = full.astype(BF16)
        low_part = (full - hi_part.astype(F32)).astype(BF16)
        for j in range(2):
            jl = slice(j * rank, (j + 1) * rank)
            ghl[2 * k + j, :levels * 8] = hi_part[:, jl]
            ghl[2 * k + j, levels * 8:] = low_part[:, jl]

    nxt = usum[...].reshape(levels * 8, half)
    for grp, (lo, hi) in ORDER:
        for l, cols in own_group(0, grp, lo, hi):
            both = jnp.dot(ghl[l], cols, preferred_element_type=F32)
            nxt = nxt + (both[:levels * 8] + both[levels * 8:])
    sv[1] = nxt.reshape(levels, 8, half)
    for l in range(levels):
        z_send(1, l)

    for grp, (lo, hi) in ORDER:
        other_group(0, grp, lo, hi)
    first = acc[...] + expand(0, levels)
    for h in range(2):
        hl = slice(h * half, (h + 1) * half)
        xs[:, hl] = (wcol[...] * first[:, hl]).astype(BF16)
    leaf_part(xs)

    z_to_gather(1)
    last = len(ORDER) - 1
    for n, (grp, (lo, hi)) in enumerate(ORDER):
        own_group(1, grp, lo, hi)
        if n >= 1:
            pgrp, (plo, phi) = ORDER[n - 1]
            other_group(1, pgrp, plo, phi)
            acc[...] += expand(plo, phi)
    grp, (lo, hi) = ORDER[last]
    other_group(1, grp, lo, hi)
    out_ref[...] = (acc[...] + expand(lo, hi)).astype(BF16)
    for ref, phase, grp in sent:
        multi_wait(ref, send_sem.at[phase, grp])


def on_device(signal, leaves, bases, couplings, weights):
    rows, width = signal.shape
    levels, _, rank = bases.shape
    count = lax.axis_size("rows")
    scales = [1.0 / math.sqrt(rows * (count >> level + 1) * rank) for level in range(levels)]
    half = width // 2
    vm = pltpu.VMEM
    anyspec = pl.BlockSpec(memory_space=pl.ANY)
    dma = pltpu.SemaphoreType.DMA

    def body(*refs):
        kernel(scales, *refs)

    return pl.pallas_call(
        body,
        name="double_product",
        out_shape=vm((rows, width), BF16),
        in_specs=[anyspec] * 5,
        out_specs=pl.BlockSpec(memory_space=vm),
        scratch_shapes=[
            vm((rows, width), BF16),
            vm((rows, levels * rank), BF16),
            vm((rows, LEAF), BF16),
            vm((levels, rank, rank), BF16),
            vm((levels, rank, rank), BF16),
            vm((rows // 128, 128), F32),
            vm((rows, 128), F32),
            vm((rows, levels * rank), BF16),
            vm((rows, width), BF16),
            vm((rows, width), BF16),
            vm((rows, width), F32),
            vm((levels * rank, width), BF16),
            vm((2, levels, rank, half), F32),
            vm((levels, rank, half), F32),
            vm((levels, rank, half), F32),
            vm((CHIPS - 1, levels, 8, half), F32),
            vm((2 * CHIPS - 1, 8, half), F32),
            vm((2, levels, rank, half), F32),
            vm((levels, rank, half), F32),
            vm((levels, rank, half), F32),
            vm((CHIPS - 1, levels, 8, half), F32),
            vm((2, levels, rank, 2 * rank), F32),
            vm((levels, rank, 2 * rank), F32),
            vm((levels, rank, 2 * rank), F32),
            vm((CHIPS - 1, levels, 8, 2 * rank), F32),
            vm((levels, 8, 2 * rank), F32),
            vm((levels, 8, 2 * rank), F32),
            vm((levels, 2 * levels * 8, rank), BF16),
            vm((levels, 8, half), F32),
            vm((2, levels, 8, half), F32),
            vm((2, PLANES, 8, half), F32),
            vm((2, levels, 8, half), F32),
            vm((2, levels, rank, half), F32),
            vm((2, levels, rank, half), F32),
            dma((16,)),
            dma((13, 4)),
            dma((13, 4)),
            pltpu.SemaphoreType.REGULAR,
        ],
        compiler_params=pltpu.CompilerParams(collective_id=0, has_side_effects=True),
    )(signal, leaves, bases, couplings, weights.reshape(rows // 128, 128))


def solution(mesh):
    in_specs = (P("rows", None), P("rows", None), P(None, "rows", None), P(), P("rows"))
    return jax.shard_map(
        on_device, mesh=mesh, in_specs=in_specs, out_specs=P("rows", None), check_vma=False
    )
```

time: 51.4 us -> 49.7 us (0.967)
  Pallas kernels: 50.5 us -> 48.8 us
    pallas_call x1, Pallas kernels: 50.5 us -> 48.8 us  [on_device(): pl.pallas_call(body, name='double_product', out_shape=vm((rows, width), B...]
where the time goes in v3:
time: 49.7 us; the launch traced here: 49.6 us
  Pallas kernels  48.8 us (98%)
  local copies, waits for them, and re-layouts  0.8 us (2%)
    pallas_call x1, Pallas kernels, on_device(): pl.pallas_call(body, name='double_product', out_shape=vm((rows, width), B...  48.8 us

profile of v3, /device:TPU:1, one launch (start us, length us, event | category | flops | bytes accessed | tf_op | source)
XLA Modules:
  0.0 49.6 jit_solution(7613138900732532953)
XLA Ops:
  0.0 48.8 %double_product.1 = bf16[1024,256]{1,0:T(8,128)(2,1)S(1)} custom-call(bf16[1024,256]{1,0:T(8,128)(2,1)} %refs_0_.1, bf16[1024,512]{1,0:T(8,128)(2,1)} %refs_1_.1, bf16[4,1024,128]{2,1,0:T(8,128)(2,1)} %refs_2_.1, bf16[15,128,128]{2,1,0:T(8,128)(2,1)} %refs_3_.1, f32[8,128]{1,0:T(8,128)} %bitcast.1), custom_call_target="tpu_custom_call" | custom-call | tf_op jit(solution)/shard_map/double_product/pallas_call | solution.py:356
  48.8 0.8 %copy.7 = bf16[1024,256]{1,0:T(8,128)(2,1)} copy(bf16[1024,256]{1,0:T(8,128)(2,1)S(1)} %double_product.1) | data formatting | bytes 1048576

commit v4 on v3

--- a/solution.py
+++ b/solution.py
@@ -246,9 +246,10 @@
         for h in range(2):
             for l in range(levels):
                 g[h, l] = got[l * rank:(l + 1) * rank, h * 2 * rank:(h + 1) * 2 * rank]
-        remote(g.at[1 - core], gbuf, PAIR_G, 0, partner)
 
     gram()
+    for l in range(levels):
+        remote(g.at[1 - core, l], gbuf.at[l], PAIR_G, l, partner)
     for grp, (lo, hi) in enumerate(GROUPS):
         if grp == 0:
             continue
@@ -256,6 +257,10 @@
         hs[lo:hi] = p[core, lo:hi] + rbuf[lo:hi]
         scatter(hs, rs, RS_P, grp, lo, hi)
 
+    for l in range(levels):
+        arrived(gbuf.at[l], PAIR_G, l)
+        gs[l] = g[core, l] + gbuf[l]
+        scatter(gs, grs, RS_G, l, l, l + 1)
     leaf_load.wait()
     leaf_part(xv)
     for h in range(2):
@@ -263,9 +268,6 @@
         ys[:, hl] = (wcol[...] * acc[:, hl]).astype(BF16)
     project(ys, u)
     remote(u.at[1 - core], ubuf, PAIR_U, 0, partner)
-    arrived(gbuf, PAIR_G, 0)
-    gs[...] = g[core] + gbuf[...]
-    scatter(gs, grs, RS_G, 0, 0, levels)
 
     know(1)
     for grp, (lo, hi) in enumerate(GROUPS):
@@ -292,10 +294,11 @@
         m = mraw[l].astype(F32)
         mor[l] = jnp.where(side == 0, m, m.T).astype(BF16)
 
-    z_to_gather(0)
-    arrived(grs, RS_G, 0)
+    for l in range(levels):
+        arrived(grs.at[:, l], RS_G, l)
     gm[...] = gathered_sum(gs, grs, 0, levels)
     remote(gm, gx, PAIR_R, 0, partner)
+    z_to_gather(0)
     arrived(urs, RS_U, 0)
     usum[...] = gathered_sum(us, urs, 0, levels)
     arrived(gx, PAIR_R, 0)

time: 49.7 us -> 49.6 us (level)
  no operation moved by 1% of the time
where the time goes in v4:
time: 49.6 us; the launch traced here: 49.4 us
  Pallas kernels  48.6 us (98%)
  local copies, waits for them, and re-layouts  0.8 us (2%)
    pallas_call x1, Pallas kernels, on_device(): pl.pallas_call(body, name='double_product', out_shape=vm((rows, width), B...  48.6 us

profile of v4, /device:TPU:1, one launch (start us, length us, event | category | flops | bytes accessed | tf_op | source)
XLA Modules:
  0.0 49.4 jit_solution(911801917837530153)
XLA Ops:
  0.0 48.6 %double_product.1 = bf16[1024,256]{1,0:T(8,128)(2,1)S(1)} custom-call(bf16[1024,256]{1,0:T(8,128)(2,1)} %refs_0_.1, bf16[1024,512]{1,0:T(8,128)(2,1)} %refs_1_.1, bf16[4,1024,128]{2,1,0:T(8,128)(2,1)} %refs_2_.1, bf16[15,128,128]{2,1,0:T(8,128)(2,1)} %refs_3_.1, f32[8,128]{1,0:T(8,128)} %bitcast.1), custom_call_target="tpu_custom_call" | custom-call | tf_op jit(solution)/shard_map/double_product/pallas_call | solution.py:359
  48.6 0.8 %copy.7 = bf16[1024,256]{1,0:T(8,128)(2,1)} copy(bf16[1024,256]{1,0:T(8,128)(2,1)S(1)} %double_product.1) | data formatting | bytes 1048576
